TPU v7x, 32 devices: a whole 2x2x4 slice. The times are simulated.
32 devices in a mesh: dp: 2 (over x), context: 4 (over z), tensor: 4 (over y, core).
Axes of the slice: x: 2, y: 2, z: 4, core: 2. Of those that a mesh axis runs over, the one named last changes fastest.
Arguments:
- tokens: bfloat16 [6144, 640], P(('dp', 'context')), may hold values from -8 to 8
- seq_lengths: int32 [2, 2], P('dp'), may hold values from 1 to 2048, 3072 in all within a row
- input_gain: bfloat16 [640], P('dp'), may hold values from 0.25 to 1.75
- query_weight: bfloat16 [640, 1024], P('dp', 'tensor'), may hold values from -0.25 to 0.25
- key_weight: bfloat16 [640, 256], P('dp'), may hold values from -0.25 to 0.25
- value_weight: bfloat16 [640, 256], P('dp'), may hold values from -0.25 to 0.25
- query_gain: bfloat16 [256], P('dp'), may hold values from 0.25 to 1.75
- key_gain: bfloat16 [256], P('dp'), may hold values from 0.25 to 1.75
- output_weight: bfloat16 [1024, 640], P('tensor', 'dp'), may hold values from -0.1875 to 0.1875
- attention_gain: bfloat16 [640], P('dp'), may hold values from 0.25 to 1.75
- prefeed_gain: bfloat16 [640], P('dp'), may hold values from 0.25 to 1.75
- gate_weight: bfloat16 [640, 2048], P('dp', 'tensor'), may hold values from -0.25 to 0.25
- up_weight: bfloat16 [640, 2048], P('dp', 'tensor'), may hold values from -0.25 to 0.25
- down_weight: bfloat16 [2048, 640], P('tensor', 'dp'), may hold values from -0.125 to 0.125
- feed_gain: bfloat16 [640], P('dp'), may hold values from 0.25 to 1.75
- cotangent: bfloat16 [6144, 640], P(('dp', 'context')), may hold values from -8 to 8
Outputs:
- layer_out: bfloat16 [6144, 640], P(('dp', 'context'))
- tokens_grad: float32 [6144, 640], P(('dp', 'context'))
- input_gain_grad: float32 [640], P('dp')
- query_weight_grad: float32 [640, 1024], P('dp', 'tensor')
- key_weight_grad: float32 [640, 256], P('dp')
- value_weight_grad: float32 [640, 256], P('dp')
- query_gain_grad: float32 [256], P('dp')
- key_gain_grad: float32 [256], P('dp')
- output_weight_grad: float32 [1024, 640], P('tensor', 'dp')
- attention_gain_grad: float32 [640], P('dp')
- prefeed_gain_grad: float32 [640], P('dp')
- gate_weight_grad: float32 [640, 2048], P('dp', 'tensor')
- up_weight_grad: float32 [640, 2048], P('dp', 'tensor')
- down_weight_grad: float32 [2048, 640], P('tensor', 'dp')
- feed_gain_grad: float32 [640], P('dp')
Inputs may be any that keep to these rules, and one draw needn't show every extreme that they name: `seq_lengths`: each row lists 2 lengths that add up to 3072, none above 2048.
All inputs are finite; a program needn't handle non-finite values.
Results may differ from a plain program's by a relative error of at most 0.022.
Values may be sent and summed in bfloat16 or wider, within the bound.
No kernel may reach another device: no remote copies, remote signals or barrier semaphores. Data moves between devices by JAX's collectives and lax.ppermute only.
A program may use at most 128 MiB of HBM per device.

v0:
```python
import math
import jax
import jax.numpy as jnp
from jax import lax
from jax.sharding import PartitionSpec as P

HD = 256
LMAX = 2048
EPS = 1e-06
NEG = -1000000000.0
SCALE = 0.0625


def passed_along(array, axis, by):
    devices = lax.axis_size(axis)
    pairs = [(i, i + by) for i in range(devices) if 0 <= i + by < devices]
    return lax.ppermute(array, axis, pairs)


def shortened(array):

    def short(part):
        return part.astype(jnp.bfloat16) if part.dtype == jnp.float32 else part

    return jax.tree.map(short, array)


def product(left_side, right_side):
    return jnp.dot(left_side, right_side, preferred_element_type=jnp.float32)


def product_lt(left_side, right_side):
    return lax.dot_general(
        left_side, right_side, (((0,), (0,)), ((), ())), preferred_element_type=jnp.float32
    )


def product_rt(left_side, right_side):
    return lax.dot_general(
        left_side, right_side, (((1,), (1,)), ((), ())), preferred_element_type=jnp.float32
    )


def rms_norm(values, scale_gain):
    return values * lax.rsqrt(jnp.mean(values * values, axis=-1, keepdims=True) + EPS) * scale_gain


def rotate(values, position):
    half_width = values.shape[-1] // 2
    frequency = jnp.exp(
        jnp.arange(half_width, dtype=jnp.float32) * (-2.0 * math.log(1000000.0) / values.shape[-1])
    )
    angles = position.astype(jnp.float32).reshape((-1,) + (1,) * (values.ndim - 1)) * frequency
    cosines = jnp.cos(angles)
    sines = jnp.sin(angles)
    first_half = values[..., :half_width]
    second_half = values[..., half_width:]
    return jnp.concatenate(
        [first_half * cosines - second_half * sines, second_half * cosines + first_half * sines],
        axis=-1,
    )


def layout(lengths, row_index):
    seq_ends = jnp.cumsum(lengths)
    starts = seq_ends - lengths
    member = (
        (row_index[:, None] >= starts[None, :]) & (row_index[:, None] < seq_ends[None, :])
    ).astype(jnp.int32)
    number = jnp.arange(lengths.shape[0], dtype=jnp.int32)
    segment = jnp.sum(member * (number[None, :] + 1), axis=1) - 1
    position = row_index - jnp.sum(member * starts[None, :], axis=1)
    return (segment, position)


def block_scores(query, key_block, allowed):
    scores = jnp.einsum("qhd,kd->hqk", query, key_block, preferred_element_type=jnp.float32) * SCALE
    return jnp.where(allowed[None], scores, NEG)


def local(
    tokens,
    seq_lengths,
    input_gain,
    query_weight,
    key_weight,
    value_weight,
    query_gain,
    key_gain,
    output_weight,
    attention_gain,
    prefeed_gain,
    gate_weight,
    up_weight,
    down_weight,
    feed_gain,
    cotangent,
):
    row_count = tokens.shape[0]
    chain_width = lax.axis_size("context")
    chain_place = lax.axis_index("context")
    chain_reach = min(chain_width - 1, (LMAX - 2) // row_count + 1)
    lengths = seq_lengths[0]
    own_index = chain_place * row_count + jnp.arange(row_count, dtype=jnp.int32)
    own_segment, own_position = layout(lengths, own_index)
    w_query, w_key, w_value, w_output, g_input, g_attention, g_query, g_key = (
        lax.all_gather(query_weight, "dp", axis=0, tiled=True),
        lax.all_gather(key_weight, "dp", axis=0, tiled=True),
        lax.all_gather(value_weight, "dp", axis=0, tiled=True),
        lax.all_gather(output_weight, "dp", axis=1, tiled=True),
        lax.all_gather(input_gain, "dp", axis=0, tiled=True),
        lax.all_gather(attention_gain, "dp", axis=0, tiled=True),
        lax.all_gather(query_gain, "dp", axis=0, tiled=True),
        lax.all_gather(key_gain, "dp", axis=0, tiled=True),
    )
    w_gate, w_up, w_down, g_prefeed, g_feed = (
        lax.all_gather(gate_weight, "dp", axis=0, tiled=True),
        lax.all_gather(up_weight, "dp", axis=0, tiled=True),
        lax.all_gather(down_weight, "dp", axis=1, tiled=True),
        lax.all_gather(prefeed_gain, "dp", axis=0, tiled=True),
        lax.all_gather(feed_gain, "dp", axis=0, tiled=True),
    )
    g_input = g_input.astype(jnp.float32)
    g_attention = g_attention.astype(jnp.float32)
    g_query = g_query.astype(jnp.float32)
    g_key = g_key.astype(jnp.float32)
    g_prefeed = g_prefeed.astype(jnp.float32)
    g_feed = g_feed.astype(jnp.float32)
    local_heads = w_query.shape[1] // HD
    stream = tokens.astype(jnp.float32)
    normed_full, input_back = jax.vjp(rms_norm, stream, g_input)
    normed = normed_full.astype(jnp.bfloat16)
    query_raw = product(normed, w_query).reshape(row_count, local_heads, HD)
    key_raw = product(normed, w_key)
    value = product(normed, w_value).astype(jnp.bfloat16)
    query_full, query_back = jax.vjp(
        lambda raw_part, gain_part: rotate(rms_norm(raw_part, gain_part), own_position),
        query_raw,
        g_query,
    )
    key_full, key_back = jax.vjp(
        lambda raw_part, gain_part: rotate(rms_norm(raw_part, gain_part), own_position),
        key_raw,
        g_key,
    )
    query = query_full.astype(jnp.bfloat16)
    key_rot = key_full.astype(jnp.bfloat16)
    blocks = []
    current = (key_rot, value)
    for step in range(chain_reach + 1):
        if step > 0:
            current = passed_along((current[0], current[1]), "context", 1)
        block_index = own_index - step * row_count
        block_segment = layout(lengths, block_index)[0]
        allowed = (own_segment[:, None] == block_segment[None, :]) & (
            block_index[None, :] <= own_index[:, None]
        )
        is_live = own_segment[0] == block_segment[row_count - 1]
        blocks.append((current[0], current[1], allowed, is_live))
    score_shape = (local_heads, row_count, row_count)
    kept_scores = []
    running_max = None
    total_mass = None
    for step in range(chain_reach + 1):
        key_block, value_block, allowed, is_live = blocks[step]

        def compute_block(key_block=key_block, allowed=allowed):
            scores = block_scores(query, key_block, allowed)
            peak = jnp.max(scores, axis=-1)
            return (scores, peak, jnp.sum(jnp.exp(scores - peak[..., None]), axis=-1))

        if step == 0:
            scores, peak, mass = compute_block()
            running_max, total_mass = (peak, mass)
        else:
            scores, peak, mass = compute_block()
            new_max = jnp.maximum(running_max, peak)
            total_mass = total_mass * jnp.exp(running_max - new_max) + mass * jnp.exp(
                peak - new_max
            )
            running_max = new_max
        kept_scores.append(scores)
    log_mass = running_max + jnp.log(total_mass)
    heads_out = jnp.zeros((row_count, local_heads, HD), jnp.float32)
    for step in range(chain_reach + 1):
        key_block, value_block, allowed, is_live = blocks[step]

        def compute_block(value_block=value_block, scores=kept_scores[step]):
            attn_probs = jnp.exp(scores - log_mass[..., None]).astype(jnp.bfloat16)
            return jnp.einsum(
                "hqk,kd->qhd", attn_probs, value_block, preferred_element_type=jnp.float32
            )

        if step == 0:
            heads_out = compute_block()
        else:
            heads_out = heads_out + compute_block()
    heads_low = heads_out.astype(jnp.bfloat16).reshape(row_count, local_heads * HD)
    attn_sum = lax.psum(product(heads_low, w_output).astype(jnp.bfloat16), "tensor").astype(
        jnp.float32
    )
    attn_post, attn_back = jax.vjp(rms_norm, attn_sum, g_attention)
    middle = stream + attn_post
    normed_feed_full, prefeed_back = jax.vjp(rms_norm, middle, g_prefeed)
    normed_feed = normed_feed_full.astype(jnp.bfloat16)
    gate_proj = product(normed_feed, w_gate)
    up_proj = product(normed_feed, w_up)
    activation, activation_back = jax.vjp(
        lambda gate_part, up_part: jax.nn.gelu(gate_part, approximate=True) * up_part,
        gate_proj,
        up_proj,
    )
    hidden = activation.astype(jnp.bfloat16)
    feed_sum = lax.psum(product(hidden, w_down).astype(jnp.bfloat16), "tensor").astype(jnp.float32)
    feed_post, feed_back = jax.vjp(rms_norm, feed_sum, g_feed)
    result = middle + feed_post
    layer_out = result.astype(jnp.bfloat16)
    grad_out = cotangent.astype(jnp.float32)
    grad_feed_full, grad_gfeed = feed_back(grad_out)
    grad_feed = grad_feed_full.astype(jnp.bfloat16)
    grad_wdown = product_lt(hidden, grad_feed)
    grad_hidden = product_rt(grad_feed, w_down)
    grad_gate_full, grad_up_full = activation_back(grad_hidden)
    grad_gate = grad_gate_full.astype(jnp.bfloat16)
    grad_up = grad_up_full.astype(jnp.bfloat16)
    grad_wgate = product_lt(normed_feed, grad_gate)
    grad_wup = product_lt(normed_feed, grad_up)
    grad_normed_feed = lax.psum(
        (product_rt(grad_gate, w_gate) + product_rt(grad_up, w_up)).astype(jnp.bfloat16), "tensor"
    ).astype(jnp.float32)
    grad_middle_norm, grad_gprefeed = prefeed_back(grad_normed_feed)
    grad_middle = grad_out + grad_middle_norm
    grad_attn_full, grad_gattention = attn_back(grad_middle)
    grad_attn = grad_attn_full.astype(jnp.bfloat16)
    grad_woutput = product_lt(heads_low, grad_attn)
    grad_heads = (
        product_rt(grad_attn, w_output).reshape(row_count, local_heads, HD).astype(jnp.bfloat16)
    )
    kept_blocks = []
    row_dots = jnp.zeros(score_shape[:2], jnp.float32)
    for step in range(chain_reach + 1):
        key_block, value_block, allowed, is_live = blocks[step]

        def compute_block(key_block=key_block, value_block=value_block, allowed=allowed):
            scores = block_scores(query, key_block, allowed)
            attn_probs = jnp.exp(scores - log_mass[..., None])
            prob_grad = jnp.einsum(
                "qhd,kd->hqk", grad_heads, value_block, preferred_element_type=jnp.float32
            )
            return (attn_probs, prob_grad, jnp.sum(attn_probs * prob_grad, axis=-1))

        if step == 0:
            attn_probs, prob_grad, partial_dots = compute_block()
        else:
            attn_probs, prob_grad, partial_dots = compute_block()
        row_dots = row_dots + partial_dots
        kept_blocks.append((attn_probs, prob_grad))
    grad_query = jnp.zeros((row_count, local_heads, HD), jnp.float32)
    carried = (jnp.zeros((row_count, HD), jnp.float32), jnp.zeros((row_count, HD), jnp.float32))
    for step in range(chain_reach, -1, -1):
        key_block, value_block, allowed, is_live = blocks[step]
        attn_probs, prob_grad = kept_blocks[step]

        def compute_block(key_block=key_block, attn_probs=attn_probs, prob_grad=prob_grad):
            grad_scores = (attn_probs * (prob_grad - row_dots[..., None])).astype(jnp.bfloat16)
            probs_low = attn_probs.astype(jnp.bfloat16)
            query_part = (
                jnp.einsum(
                    "hqk,kd->qhd", grad_scores, key_block, preferred_element_type=jnp.float32
                )
                * SCALE
            )
            key_part = (
                jnp.einsum("hqk,qhd->kd", grad_scores, query, preferred_element_type=jnp.float32)
                * SCALE
            )
            value_part = jnp.einsum(
                "hqk,qhd->kd", probs_low, grad_heads, preferred_element_type=jnp.float32
            )
            return (query_part, key_part, value_part)

        if step == 0:
            query_part, key_part, value_part = compute_block()
        else:
            query_part, key_part, value_part = compute_block()
        grad_query = grad_query + query_part
        carried = (carried[0] + key_part, carried[1] + value_part)
        if step > 0:
            carried = passed_along((shortened(carried[0]), shortened(carried[1])), "context", -1)
    grad_key, grad_value = (
        lax.psum(carried[0].astype(jnp.bfloat16), "tensor").astype(jnp.float32),
        lax.psum(carried[1].astype(jnp.bfloat16), "tensor").astype(jnp.float32),
    )
    grad_query_full, grad_gquery_part = query_back(grad_query)
    grad_key_full, grad_gkey = key_back(grad_key)
    grad_query_raw = grad_query_full.reshape(row_count, local_heads * HD).astype(jnp.bfloat16)
    grad_key_raw = grad_key_full.astype(jnp.bfloat16)
    grad_value_low = grad_value.astype(jnp.bfloat16)
    grad_wquery = product_lt(normed, grad_query_raw)
    grad_wkey = product_lt(normed, grad_key_raw)
    grad_wvalue = product_lt(normed, grad_value_low)
    grad_normed_part = product_rt(grad_query_raw, w_query)
    grad_normed_sum, grad_gquery = (
        lax.psum(grad_normed_part.astype(jnp.bfloat16), "tensor").astype(jnp.float32),
        lax.psum(grad_gquery_part.astype(jnp.bfloat16), "tensor").astype(jnp.float32),
    )
    grad_normed = (
        grad_normed_sum + product_rt(grad_key_raw, w_key) + product_rt(grad_value_low, w_value)
    )
    grad_stream_norm, grad_ginput = input_back(grad_normed)
    tokens_grad = grad_middle + grad_stream_norm
    totals = lax.psum(
        (
            grad_ginput,
            grad_wquery,
            grad_wkey,
            grad_wvalue,
            grad_gquery,
            grad_gkey,
            grad_woutput,
            grad_gattention,
            grad_gprefeed,
            grad_wgate,
            grad_wup,
            grad_wdown,
            grad_gfeed,
        ),
        ("dp", "context"),
    )
    shard_place = lax.axis_index("dp")
    shard_count = lax.axis_size("dp")
    slice_dims = (0, 0, 0, 0, 0, 0, 1, 0, 0, 0, 0, 1, 0)
    shares = tuple(
        (
            lax.dynamic_slice_in_dim(
                total_grad,
                shard_place * (total_grad.shape[dim_index] // shard_count),
                total_grad.shape[dim_index] // shard_count,
                dim_index,
            )
            for total_grad, dim_index in zip(totals, slice_dims)
        )
    )
    return (
        layer_out,
        tokens_grad,
        shares[0],
        shares[1],
        shares[2],
        shares[3],
        shares[4],
        shares[5],
        shares[6],
        shares[7],
        shares[8],
        shares[9],
        shares[10],
        shares[11],
        shares[12],
    )


def solution(mesh):
    placed = (
        P(("dp", "context"), None),
        P("dp", None),
        P("dp"),
        P("dp", "tensor"),
        P("dp", None),
        P("dp", None),
        P("dp"),
        P("dp"),
        P("tensor", "dp"),
        P("dp"),
        P("dp"),
        P("dp", "tensor"),
        P("dp", "tensor"),
        P("tensor", "dp"),
        P("dp"),
        P(("dp", "context"), None),
    )
    return jax.shard_map(
        local,
        mesh=mesh,
        in_specs=placed,
        out_specs=(
            P(("dp", "context"), None),
            P(("dp", "context"), None),
            P("dp"),
            P("dp", "tensor"),
            P("dp", None),
            P("dp", None),
            P("dp"),
            P("dp"),
            P("tensor", "dp"),
            P("dp"),
            P("dp"),
            P("dp", "tensor"),
            P("dp", "tensor"),
            P("tensor", "dp"),
            P("dp"),
        ),
        check_vma=False,
    )
```

profile of v0, /device:TPU:0, one launch (start us, length us, event | category | flops | bytes accessed | tf_op | source)
XLA Modules:
  0.0 614.7 jit_solution(17788061807862818543)
XLA Ops:
  12.6 6.5 %all-reduce.11 = (bf16[640]{0:T(1024)(128)(2,1)S(1)}, bf16[640]{0:T(1024)(128)(2,1)S(1)}, bf16[640]{0:T(1024)(128)(2,1)S(1)}, bf16[640]{0:T(1024)(128)(2,1)}) all-reduce(bf16[640]{0:T(1024)(128)(2,1)S(1)} %dynamic-update-slice.2, bf16[640]{0:T(1024)(128)(2,1)S(1)} %dynamic-update-slice.1, ...), channel_id=1, replica_groups=mesh['dp'=2,'context'=4,'tensor'=4] {'dp'}, use_global_device_ids=true, to_apply=%add.6 | all-reduce | flops 2560 | bytes 10240
  20.6 6.4 %all_gather.40 = bf16[640,256]{1,0:T(8,128)(2,1)S(1)} all-gather(bf16[320,256]{1,0:T(8,128)(2,1)} %param.21), channel_id=1, replica_groups=mesh['dp'=2,'context'=4,'tensor'=4] {'dp'}, dimensions={0}, use_global_device_ids=true | all-gather | bytes 491520 | tf_op jit(solution)/shard_map/all_gather | solution.py:109
  29.5 4.0 collective-permute-start.3
  33.8 4.2 all-gather
  38.1 6.0 all_gather.41
  47.3 3.5 collective-permute-start
  50.8 4.2 all-gather.1
  55.6 6.0 all_gather.43
  61.6 6.0 all_gather.45
  78.0 6.2 %collective-permute-done.4 = bf16[768,256]{1,0:T(8,128)(2,1)S(1)} collective-permute-done((bf16[768,256]{1,0:T(8,128)(2,1)S(1)}, bf16[768,256]{1,0:T(8,128)(2,1)S(1)}, u32[]{:S(2)}, u32[]{:S(2)}) %collective-permute-start.4) | collective-permute-done | bytes 393248 | tf_op jit(solution)/shard_map/ppermute | solution.py:17
  84.3 4.4 collective-permute-start.5
  92.1 4.9 collective-permute-start.2
  98.1 3.6 collective-permute-done.2
  109.4 9.3 %all_gather.48 = bf16[640,512]{1,0:T(8,128)(2,1)} all-gather(bf16[320,512]{1,0:T(8,128)(2,1)} %param.27), channel_id=1, replica_groups=mesh['dp'=2,'context'=4,'tensor'=4] {'dp'}, dimensions={0}, use_global_device_ids=true | all-gather | bytes 983040 | tf_op jit(solution)/shard_map/all_gather | solution.py:117
  118.7 9.2 %all_gather.49 = bf16[640,512]{1,0:T(8,128)(2,1)} all-gather(bf16[320,512]{1,0:T(8,128)(2,1)} %param.28), channel_id=1, replica_groups=mesh['dp'=2,'context'=4,'tensor'=4] {'dp'}, dimensions={0}, use_global_device_ids=true | all-gather | bytes 983040 | tf_op jit(solution)/shard_map/all_gather | solution.py:118
  127.9 7.8 %all_gather.50 = bf16[512,640]{0,1:T(8,128)(2,1)} all-gather(bf16[512,320]{0,1:T(8,128)(2,1)S(1)} %copy-done.67), channel_id=1, replica_groups=mesh['dp'=2,'context'=4,'tensor'=4] {'dp'}, dimensions={1}, use_global_device_ids=true | all-gather | bytes 983040 | tf_op jit(solution)/shard_map/all_gather | solution.py:119
  135.8 9.4 %all-reduce.18.cloned.1.call-done = bf16[768,640]{1,0:T(8,128)(2,1)} async-done(((bf16[768,640]{1,0:T(8,128)(2,1)}), bf16[768,640]{1,0:T(8,128)(2,1)}) %all-reduce.18.cloned.1.call-update) | async-done | bytes 983056 | tf_op jit(solution)/shard_map/psum | solution.py:199
  158.8 34.7 %all-reduce.20.cloned.1.call-done = bf16[768,640]{1,0:T(8,128)(2,1)} async-done(((bf16[768,640]{1,0:T(8,128)(2,1)}), bf16[768,640]{1,0:T(8,128)(2,1)}) %all-reduce.20.cloned.1.call-update) | async-done | bytes 983056 | tf_op jit(solution)/shard_map/psum | solution.py:214
  208.9 32.5 %all-reduce.22.cloned.1.call-done = bf16[768,640]{1,0:T(8,128)(2,1)} async-done(((bf16[768,640]{1,0:T(8,128)(2,1)}), bf16[768,640]{1,0:T(8,128)(2,1)}) %all-reduce.22.cloned.1.call-update) | async-done | bytes 983056 | tf_op jit(solution)/shard_map/psum | solution.py:228
  241.5 3.5 fusion.26
  245.0 4.3 fusion.24
  273.2 6.4 %collective-permute-done.9 = bf16[768,256]{1,0:T(8,128)(2,1)S(1)} collective-permute-done((bf16[768,256]{1,0:T(8,128)(2,1)S(1)}, bf16[768,256]{1,0:T(8,128)(2,1)S(1)}, u32[]{:S(2)}, u32[]{:S(2)}) %collective-permute-start.9) | collective-permute-done | bytes 393248 | tf_op jit(solution)/shard_map/ppermute | solution.py:17
  281.4 6.6 %collective-permute-done.6 = bf16[768,256]{0,1:T(8,128)(2,1)S(1)} collective-permute-done((bf16[768,256]{0,1:T(8,128)(2,1)S(1)}, bf16[768,256]{0,1:T(8,128)(2,1)S(1)}, u32[]{:S(2)}, u32[]{:S(2)}) %collective-permute-start.6) | collective-permute-done | bytes 393248 | tf_op jit(solution)/shard_map/ppermute | solution.py:17
  290.0 6.4 %collective-permute-done.10 = bf16[768,256]{1,0:T(8,128)(2,1)S(1)} collective-permute-done((bf16[768,256]{1,0:T(8,128)(2,1)S(1)}, bf16[768,256]{1,0:T(8,128)(2,1)S(1)}, u32[]{:S(2)}, u32[]{:S(2)}) %collective-permute-start.10) | collective-permute-done | bytes 393248 | tf_op jit(solution)/shard_map/ppermute | solution.py:17
  297.8 7.0 %collective-permute-done.7 = bf16[768,256]{0,1:T(8,128)(2,1)S(1)} collective-permute-done((bf16[768,256]{0,1:T(8,128)(2,1)S(1)}, bf16[768,256]{0,1:T(8,128)(2,1)S(1)}, u32[]{:S(2)}, u32[]{:S(2)}) %collective-permute-start.7) | collective-permute-done | bytes 393248 | tf_op jit(solution)/shard_map/ppermute | solution.py:17
  307.7 5.5 collective-permute-done.11
  314.1 5.6 collective-permute-done.8
  328.2 39.0 %all-reduce.26.cloned.1.call-done = (bf16[768,256]{0,1:T(8,128)(2,1)}, bf16[768,640]{1,0:T(8,128)(2,1)}, bf16[768,256]{1,0:T(8,128)(2,1)}) async-done(((bf16[768,256]{0,1:T(8,128)(2,1)}, bf16[768,640]{1,0:T(8,128)(2,1)}, bf16[768,256]{1,0:T(8,128)(2,1)}), (bf16[768,256]{0,1:T(8,128)(2,1)}, bf16[768,640]{1,0:T(8,128)(2,1)}, bf16[768,256]{1,0:T(8,128)(2,1)})) %all-reduce.26.cloned.1.call-update) | async-done | bytes 1769488 | tf_op jit(solution)/shard_map/psum | solution.py:291
  373.3 5.9 psum.150
  379.8 3.7 fusion.21
  383.5 40.1 %all-reduce.8 = (f32[640]{0:T(1024)S(1)}, f32[256]{0:T(256)S(1)}, f32[256]{0:T(256)S(1)}, f32[640]{0:T(1024)S(1)}, f32[640]{0:T(1024)S(1)}, /*index=5*/f32[640]{0:T(1024)S(1)}) all-reduce(f32[640]{0:T(1024)S(1)} %get-tuple-element.19, bf16[256]{0:T(256)(128)(2,1)S(1)} %psum.150, ...), channel_id=1, replica_groups=mesh['dp'=2,'context'=4,'tensor'=4] {'dp','context'}, use_global_device_ids=true, to_apply=%region_37.38 | all-reduce | flops 3072 | bytes 24064 | tf_op jit(solution)/shard_map/psum | solution.py:312
  430.7 168.4 %all-reduce.24.cloned.1.call-done = (f32[640,256]{1,0:T(8,128)}, f32[640,256]{1,0:T(8,128)}, f32[640,256]{1,0:T(8,128)}, f32[256,640]{0,1:T(8,128)}, f32[640,512...) async-done(((f32[640,256]{1,0:T(8,128)}, f32[640,256]{1,0:T(8,128)}, f32[640,256]{1,0:T(8,128)}, f32[256,640]{0,1:T(8,128)}, f32[640,512]{1,0:T(8,128)}, ...) | async-done | bytes 6553616 | tf_op jit(solution)/shard_map/psum | solution.py:312
  (392 shorter events, 127.0 us)
Async XLA Ops:
  7.2 138.0 %all-reduce.18.cloned.1.call-start = ((), (), s32[]{:S(2)}) async-start(), calls=%async_computation | async-start | bytes 1966080 | tf_op jit(solution)/shard_map/psum | solution.py:199
  19.0 48.6 %copy-start.87 = (f32[640]{0:T(1024)}, f32[640]{0:T(1024)S(1)}, u32[]{:S(2)}) copy-start(f32[640]{0:T(1024)S(1)} %convert_element_type.203) | copy-start | bytes 7684
  20.6 24.2 %copy-start.91 = (f32[768]{0:T(1024)}, f32[768]{0:T(1024)S(1)}, u32[]{:S(2)}) copy-start(f32[768]{0:T(1024)S(1)} %fusion.35) | copy-start | bytes 9220
  20.6 47.0 %copy-start.89 = (f32[768]{0:T(1024)}, f32[768]{0:T(1024)S(1)}, u32[]{:S(2)}) copy-start(f32[768]{0:T(1024)S(1)} %fusion.124) | copy-start | bytes 9220
  29.5 41.9 %collective-permute-start.3 = (bf16[768,256]{1,0:T(8,128)(2,1)S(1)}, bf16[768,256]{1,0:T(8,128)(2,1)S(1)}, u32[]{:S(2)}, u32[]{:S(2)}) collective-permute-start(bf16[768,256]{1,0:T(8,128)(2,1)S(1)} %convolution_convert_fusion.5), channel_id=1, source_target_pairs={{0,4},{4,8},{8,12},{1,5},{5,9},{9,13},{2,6},{6,10},{10,14},{3,7},{... | collective-permute-start | bytes 1179656 | tf_op jit(solution)/shard_map/ppermute | solution.py:17
  33.5 35.0 %copy-start.114 = (f32[128]{0:T(128)}, f32[128]{0:T(128)S(1)}, u32[]{:S(2)}) copy-start(f32[128]{0:T(128)S(1)} %multiply_exponential_fusion) | copy-start | bytes 1540
  33.6 43.3 %copy-start.108 = (s32[768]{0:T(1024)}, s32[768]{0:T(1024)S(1)}, u32[]{:S(2)}) copy-start(s32[768]{0:T(1024)S(1)} %get-tuple-element.88) | copy-start | bytes 9220
  47.3 27.6 %collective-permute-start = (bf16[768,256]{0,1:T(8,128)(2,1)S(1)}, bf16[768,256]{0,1:T(8,128)(2,1)S(1)}, u32[]{:S(2)}, u32[]{:S(2)}) collective-permute-start(bf16[768,256]{0,1:T(8,128)(2,1)S(1)} %pad_maximum_fusion), channel_id=1, source_target_pairs={{0,4},{4,8},{8,12},{1,5},{5,9},{9,13},{2,6},{6,10},{10,14},{3,7},{... | collective-permute-start | bytes 1179656 | tf_op jit(solution)/shard_map/ppermute | solution.py:17
  67.6 39.3 %copy-start.27 = (bf16[256,640]{0,1:T(8,128)(2,1)}, bf16[256,640]{0,1:T(8,128)(2,1)S(1)}, u32[]{:S(2)}) copy-start(bf16[256,640]{0,1:T(8,128)(2,1)S(1)} %all_gather.45) | copy-start | bytes 983044
  70.2 31.6 %copy-start.68 = (bf16[768,128]{0,1:T(8,128)(2,1)}, bf16[768,128]{0,1:T(8,128)(2,1)S(1)}, u32[]{:S(2)}) copy-start(bf16[768,128]{0,1:T(8,128)(2,1)S(1)} %get-tuple-element.64) | copy-start | bytes 589828
  70.2 31.6 %copy-start.70 = (bf16[768,128]{0,1:T(8,128)(2,1)}, bf16[768,128]{0,1:T(8,128)(2,1)S(1)}, u32[]{:S(2)}) copy-start(bf16[768,128]{0,1:T(8,128)(2,1)S(1)} %get-tuple-element.65) | copy-start | bytes 589828
  71.0 32.7 %copy-start = (f32[1,768,768]{1,2,0:T(8,128)}, f32[1,768,768]{1,2,0:T(8,128)S(1)}, u32[]{:S(2)}) copy-start(f32[1,768,768]{1,2,0:T(8,128)S(1)} %get-tuple-element.83) | copy-start | bytes 7077892
  71.4 12.9 %collective-permute-start.4 = (bf16[768,256]{1,0:T(8,128)(2,1)S(1)}, bf16[768,256]{1,0:T(8,128)(2,1)S(1)}, u32[]{:S(2)}, u32[]{:S(2)}) collective-permute-start(bf16[768,256]{1,0:T(8,128)(2,1)S(1)} %collective-permute-done.3), channel_id=1, source_target_pairs={{0,4},{4,8},{8,12},{1,5},{5,9},{9,13},{2,6},{6,10},{10,14},{3,7},{... | collective-permute-start | bytes 1179656 | tf_op jit(solution)/shard_map/ppermute | solution.py:17
  74.9 17.2 %collective-permute-start.1 = (bf16[768,256]{0,1:T(8,128)(2,1)S(1)}, bf16[768,256]{0,1:T(8,128)(2,1)S(1)}, u32[]{:S(2)}, u32[]{:S(2)}) collective-permute-start(bf16[768,256]{0,1:T(8,128)(2,1)S(1)} %collective-permute-done), channel_id=1, source_target_pairs={{0,4},{4,8},{8,12},{1,5},{5,9},{9,13},{2,6},{6,10},{10,14},{3,7},{... | collective-permute-start | bytes 1179656 | tf_op jit(solution)/shard_map/ppermute | solution.py:17
  77.6 27.5 %copy-start.2 = (f32[1,768,768]{1,2,0:T(8,128)}, f32[1,768,768]{1,2,0:T(8,128)S(1)}, u32[]{:S(2)}) copy-start(f32[1,768,768]{1,2,0:T(8,128)S(1)} %get-tuple-element.81) | copy-start | bytes 7077892
  84.3 22.0 %collective-permute-start.5 = (bf16[768,256]{1,0:T(8,128)(2,1)S(1)}, bf16[768,256]{1,0:T(8,128)(2,1)S(1)}, u32[]{:S(2)}, u32[]{:S(2)}) collective-permute-start(bf16[768,256]{1,0:T(8,128)(2,1)S(1)} %collective-permute-done.4), channel_id=1, source_target_pairs={{0,4},{4,8},{8,12},{1,5},{5,9},{9,13},{2,6},{6,10},{10,14},{3,7},{... | collective-permute-start | bytes 1179656 | tf_op jit(solution)/shard_map/ppermute | solution.py:17
  92.1 9.7 %collective-permute-start.2 = (bf16[768,256]{0,1:T(8,128)(2,1)S(1)}, bf16[768,256]{0,1:T(8,128)(2,1)S(1)}, u32[]{:S(2)}, u32[]{:S(2)}) collective-permute-start(bf16[768,256]{0,1:T(8,128)(2,1)S(1)} %collective-permute-done.1), channel_id=1, source_target_pairs={{0,4},{4,8},{8,12},{1,5},{5,9},{9,13},{2,6},{6,10},{10,14},{3,7},{... | collective-permute-start | bytes 1179656 | tf_op jit(solution)/shard_map/ppermute | solution.py:17
  109.3 84.3 %all-reduce.20.cloned.1.call-start = ((), (), s32[]{:S(2)}) async-start(), calls=%async_computation.1 | async-start | bytes 1966080 | tf_op jit(solution)/shard_map/psum | solution.py:214
  157.5 83.9 %all-reduce.22.cloned.1.call-start = ((), (), s32[]{:S(2)}) async-start(), calls=%async_computation.2 | async-start | bytes 1966080 | tf_op jit(solution)/shard_map/psum | solution.py:228
  205.4 161.8 %all-reduce.26.cloned.1.call-start = ((), (), s32[]{:S(2)}) async-start(), calls=%async_computation.4 | async-start | bytes 3538944 | tf_op jit(solution)/shard_map/psum | solution.py:291
  265.6 13.9 %collective-permute-start.9 = (bf16[768,256]{1,0:T(8,128)(2,1)S(1)}, bf16[768,256]{1,0:T(8,128)(2,1)S(1)}, u32[]{:S(2)}, u32[]{:S(2)}) collective-permute-start(bf16[768,256]{1,0:T(8,128)(2,1)S(1)} %convolution_convert_fusion.3), channel_id=1, source_target_pairs={{4,0},{8,4},{12,8},{5,1},{9,5},{13,9},{6,2},{10,6},{14,10},{7,3},{... | collective-permute-start | bytes 1179656 | tf_op jit(solution)/shard_map/ppermute | solution.py:17
  271.3 16.7 %collective-permute-start.6 = (bf16[768,256]{0,1:T(8,128)(2,1)S(1)}, bf16[768,256]{0,1:T(8,128)(2,1)S(1)}, u32[]{:S(2)}, u32[]{:S(2)}) collective-permute-start(bf16[768,256]{0,1:T(8,128)(2,1)S(1)} %fusion.53), channel_id=1, source_target_pairs={{4,0},{8,4},{12,8},{5,1},{9,5},{13,9},{6,2},{10,6},{14,10},{7,3},{... | collective-permute-start | bytes 1179656 | tf_op jit(solution)/shard_map/ppermute | solution.py:17
  280.1 16.3 %collective-permute-start.10 = (bf16[768,256]{1,0:T(8,128)(2,1)S(1)}, bf16[768,256]{1,0:T(8,128)(2,1)S(1)}, u32[]{:S(2)}, u32[]{:S(2)}) collective-permute-start(bf16[768,256]{1,0:T(8,128)(2,1)S(1)} %add_convert_fusion.3), channel_id=1, source_target_pairs={{4,0},{8,4},{12,8},{5,1},{9,5},{13,9},{6,2},{10,6},{14,10},{7,3},{... | collective-permute-start | bytes 1179656 | tf_op jit(solution)/shard_map/ppermute | solution.py:17
  288.5 16.3 %collective-permute-start.7 = (bf16[768,256]{0,1:T(8,128)(2,1)S(1)}, bf16[768,256]{0,1:T(8,128)(2,1)S(1)}, u32[]{:S(2)}, u32[]{:S(2)}) collective-permute-start(bf16[768,256]{0,1:T(8,128)(2,1)S(1)} %add_convert_fusion.6), channel_id=1, source_target_pairs={{4,0},{8,4},{12,8},{5,1},{9,5},{13,9},{6,2},{10,6},{14,10},{7,3},{... | collective-permute-start | bytes 1179656 | tf_op jit(solution)/shard_map/ppermute | solution.py:17
  296.5 16.8 %collective-permute-start.11 = (bf16[768,256]{1,0:T(8,128)(2,1)S(1)}, bf16[768,256]{1,0:T(8,128)(2,1)S(1)}, u32[]{:S(2)}, u32[]{:S(2)}) collective-permute-start(bf16[768,256]{1,0:T(8,128)(2,1)S(1)} %add_convert_fusion.2), channel_id=1, source_target_pairs={{4,0},{8,4},{12,8},{5,1},{9,5},{13,9},{6,2},{10,6},{14,10},{7,3},{... | collective-permute-start | bytes 1179656 | tf_op jit(solution)/shard_map/ppermute | solution.py:17
  304.9 14.8 %collective-permute-start.8 = (bf16[768,256]{0,1:T(8,128)(2,1)S(1)}, bf16[768,256]{0,1:T(8,128)(2,1)S(1)}, u32[]{:S(2)}, u32[]{:S(2)}) collective-permute-start(bf16[768,256]{0,1:T(8,128)(2,1)S(1)} %add_convert_fusion.5), channel_id=1, source_target_pairs={{4,0},{8,4},{12,8},{5,1},{9,5},{13,9},{6,2},{10,6},{14,10},{7,3},{... | collective-permute-start | bytes 1179656 | tf_op jit(solution)/shard_map/ppermute | solution.py:17
  320.6 278.6 %all-reduce.24.cloned.1.call-start = ((), (), s32[]{:S(2)}) async-start(), calls=%async_computation.3 | async-start | bytes 13107200 | tf_op jit(solution)/shard_map/psum | solution.py:312
  328.2 41.7 %copy-start.18 = (f32[768,256]{0,1:T(8,128)S(1)}, f32[768,256]{0,1:T(8,128)}, u32[]{:S(2)}) copy-start(f32[768,256]{0,1:T(8,128)} %copy-done.17) | copy-start | bytes 2359300
  328.2 41.7 %copy-start.84 = (f32[768]{0:T(1024)S(1)}, f32[768]{0:T(1024)}, u32[]{:S(2)}) copy-start(f32[768]{0:T(1024)} %copy-done.83) | copy-start | bytes 9220
  328.2 41.7 %copy-start.99 = (f32[2,1,128]{2,1,0:T(1,128)S(1)}, f32[2,1,128]{2,1,0:T(1,128)}, u32[]{:S(2)}) copy-start(f32[2,1,128]{2,1,0:T(1,128)} %copy-done.98) | copy-start | bytes 3076
  379.8 47.6 %copy-start.92 = (f32[768]{0:T(1024)S(1)}, f32[768]{0:T(1024)}, u32[]{:S(2)}) copy-start(f32[768]{0:T(1024)} %copy-done.91) | copy-start | bytes 9220
  379.8 47.6 %copy-start.10 = (f32[768,640]{1,0:T(8,128)S(1)}, f32[768,640]{1,0:T(8,128)}, u32[]{:S(2)}) copy-start(f32[768,640]{1,0:T(8,128)} %copy-done.9) | copy-start | bytes 5898244
  (106 other events, 557.1 us)
Sparse Core Ops, SparseCore 0:
  109.4 35.7 all-reduce.17
  157.6 35.9 all-reduce.19
  205.5 35.8 all-reduce.21
  320.7 46.4 all-reduce.25
  373.4 225.6 all-reduce.23
where the time goes:
time: 623 us; the launch traced here: 615 us
  waiting for transfers between devices  335 us (54%)
  blocking collectives  112 us (18%)
  matrix products  48.5 us (8%)
  other arithmetic  39.9 us (6%)
  local copies, waits for them, and re-layouts  32.8 us (5%)
  starting transfers between devices  30.5 us (5%)
  between operations  16.3 us (3%)
    psum x1, waiting for transfers between devices, local(): lax.psum((grad_ginput, grad_wquery, grad_wkey, grad_wvalue, grad_gquery,...  168 us
    ppermute x12, waiting for transfers between devices, passed_along(): return lax.ppermute(array, axis, pairs)  50.9 us
    psum x1, blocking collectives, local(): lax.psum((grad_ginput, grad_wquery, grad_wkey, grad_wvalue, grad_gquery,...  40.1 us
    psum x1, waiting for transfers between devices, local(): lax.psum(carried[0].astype(jnp.bfloat16), 'tensor').astype(jnp.float32)  39 us
    psum x1, waiting for transfers between devices, local(): lax.psum(product(hidden, w_down).astype(jnp.bfloat16), 'tensor')  34.7 us
    psum x1, waiting for transfers between devices, local(): lax.psum((product_rt(grad_gate, w_gate) + product_rt(grad_up, w_up)).asty...  32.5 us
    ppermute x12, starting transfers between devices, passed_along(): return lax.ppermute(array, axis, pairs)  30.1 us
    unnamed x251, local copies, waits for them, and re-layouts  20.3 us
  transfers between devices with their start and end apart: 17, of which 14 were waited for; matrix products, arithmetic and copies ran while one was open for 7% of the time, Pallas kernels for 0%

commit v1 on v0

--- a/solution.py
+++ b/solution.py
@@ -310,22 +310,25 @@
     grad_stream_norm, grad_ginput = input_back(grad_normed)
     tokens_grad = grad_middle + grad_stream_norm
     totals = lax.psum(
-        (
-            grad_ginput,
-            grad_wquery,
-            grad_wkey,
-            grad_wvalue,
-            grad_gquery,
-            grad_gkey,
-            grad_woutput,
-            grad_gattention,
-            grad_gprefeed,
-            grad_wgate,
-            grad_wup,
-            grad_wdown,
-            grad_gfeed,
+        lax.psum(
+            (
+                grad_ginput,
+                grad_wquery,
+                grad_wkey,
+                grad_wvalue,
+                grad_gquery,
+                grad_gkey,
+                grad_woutput,
+                grad_gattention,
+                grad_gprefeed,
+                grad_wgate,
+                grad_wup,
+                grad_wdown,
+                grad_gfeed,
+            ),
+            "context",
         ),
-        ("dp", "context"),
+        "dp",
     )
     shard_place = lax.axis_index("dp")
     shard_count = lax.axis_size("dp")

time: 623 us -> 794 us (1.27)
  waiting for transfers between devices: 335 us -> 520 us
  blocking collectives: 112 us -> 98 us
    psum x0 -> x1, waiting for transfers between devices: none -> 119 us  [local(): lax.psum(lax.psum((grad_ginput, grad_wquery, grad_wkey, grad_wvalue, grad...]
    psum x1, waiting for transfers between devices: 168 us -> 234 us  [local(): lax.psum((grad_ginput, grad_wquery, grad_wkey, grad_wvalue, grad_gquery,...]
    psum x1, blocking collectives: 40.1 us -> 16.7 us  [local(): lax.psum((grad_ginput, grad_wquery, grad_wkey, grad_wvalue, grad_gquery,...]
    psum x0 -> x1, blocking collectives: none -> 8.64 us  [local(): lax.psum(lax.psum((grad_ginput, grad_wquery, grad_wkey, grad_wvalue, grad...]
  transfers between devices with their start and end apart: 17 -> 18, of which waited for: 14 -> 15; matrix products, arithmetic and copies ran while one was open for 7% -> 6% of each run, Pallas kernels for 0% -> 0%
where the time goes in v1:
time: 794 us; the launch traced here: 786 us
  waiting for transfers between devices  520 us (65%)
  blocking collectives  98 us (12%)
  matrix products  48.8 us (6%)
  other arithmetic  39.9 us (5%)
  local copies, waits for them, and re-layouts  32.8 us (4%)
  starting transfers between devices  30.6 us (4%)
  between operations  16.7 us (2%)
    psum x1, waiting for transfers between devices, local(): lax.psum((grad_ginput, grad_wquery, grad_wkey, grad_wvalue, grad_gquery,...  234 us
    psum x1, waiting for transfers between devices, local(): lax.psum(lax.psum((grad_ginput, grad_wquery, grad_wkey, grad_wvalue, grad...  119 us
    ppermute x12, waiting for transfers between devices, passed_along(): return lax.ppermute(array, axis, pairs)  50.9 us
    psum x1, waiting for transfers between devices, local(): lax.psum(carried[0].astype(jnp.bfloat16), 'tensor').astype(jnp.float32)  38.8 us
    psum x1, waiting for transfers between devices, local(): lax.psum(product(hidden, w_down).astype(jnp.bfloat16), 'tensor')  34.7 us
    psum x1, waiting for transfers between devices, local(): lax.psum((product_rt(grad_gate, w_gate) + product_rt(grad_up, w_up)).asty...  32.5 us
    ppermute x12, starting transfers between devices, passed_along(): return lax.ppermute(array, axis, pairs)  30.1 us
    unnamed x251, local copies, waits for them, and re-layouts  20.3 us
  transfers between devices with their start and end apart: 18, of which 15 were waited for; matrix products, arithmetic and copies ran while one was open for 6% of the time, Pallas kernels for 0%

profile of v1, /device:TPU:0, one launch (start us, length us, event | category | flops | bytes accessed | tf_op | source)
XLA Modules:
  0.0 786.2 jit_solution(8025184135944303783)
XLA Ops:
  12.6 6.5 all-reduce.13
  20.6 6.4 all_gather.40
  29.5 4.0 collective-permute-start.3
  33.8 4.2 all-gather
  38.1 6.0 all_gather.41
  50.8 4.2 all-gather.1
  55.6 6.0 all_gather.43
  61.6 6.0 all_gather.45
  78.0 6.2 collective-permute-done.4
  84.3 4.4 collective-permute-start.5
  92.1 4.9 collective-permute-start.2
  98.1 3.6 collective-permute-done.2
  109.4 9.3 %all_gather.48 = bf16[640,512]{1,0:T(8,128)(2,1)} all-gather(bf16[320,512]{1,0:T(8,128)(2,1)} %param.27), channel_id=1, replica_groups=mesh['dp'=2,'context'=4,'tensor'=4] {'dp'}, dimensions={0}, use_global_device_ids=true | all-gather | bytes 983040 | tf_op jit(solution)/shard_map/all_gather | solution.py:117
  118.7 9.2 %all_gather.49 = bf16[640,512]{1,0:T(8,128)(2,1)} all-gather(bf16[320,512]{1,0:T(8,128)(2,1)} %param.28), channel_id=1, replica_groups=mesh['dp'=2,'context'=4,'tensor'=4] {'dp'}, dimensions={0}, use_global_device_ids=true | all-gather | bytes 983040 | tf_op jit(solution)/shard_map/all_gather | solution.py:118
  127.9 7.8 all_gather.50
  135.8 9.4 %all-reduce.21.cloned.1.call-done = bf16[768,640]{1,0:T(8,128)(2,1)} async-done(((bf16[768,640]{1,0:T(8,128)(2,1)}), bf16[768,640]{1,0:T(8,128)(2,1)}) %all-reduce.21.cloned.1.call-update) | async-done | bytes 983056 | tf_op jit(solution)/shard_map/psum | solution.py:199
  158.8 34.7 %all-reduce.23.cloned.1.call-done = bf16[768,640]{1,0:T(8,128)(2,1)} async-done(((bf16[768,640]{1,0:T(8,128)(2,1)}), bf16[768,640]{1,0:T(8,128)(2,1)}) %all-reduce.23.cloned.1.call-update) | async-done | bytes 983056 | tf_op jit(solution)/shard_map/psum | solution.py:214
  208.9 32.5 %all-reduce.25.cloned.1.call-done = bf16[768,640]{1,0:T(8,128)(2,1)} async-done(((bf16[768,640]{1,0:T(8,128)(2,1)}), bf16[768,640]{1,0:T(8,128)(2,1)}) %all-reduce.25.cloned.1.call-update) | async-done | bytes 983056 | tf_op jit(solution)/shard_map/psum | solution.py:228
  245.0 4.3 fusion.24
  273.2 6.4 collective-permute-done.9
  281.4 6.6 collective-permute-done.6
  290.0 6.4 collective-permute-done.10
  297.8 7.0 collective-permute-done.7
  307.7 5.6 collective-permute-done.11
  314.1 5.6 collective-permute-done.8
  328.3 38.8 %all-reduce.31.cloned.1.call-done = (bf16[768,256]{0,1:T(8,128)(2,1)}, bf16[768,640]{1,0:T(8,128)(2,1)}, bf16[768,256]{1,0:T(8,128)(2,1)}) async-done(((bf16[768,256]{0,1:T(8,128)(2,1)}, bf16[768,640]{1,0:T(8,128)(2,1)}, bf16[768,256]{1,0:T(8,128)(2,1)}), (bf16[768,256]{0,1:T(8,128)(2,1)}, bf16[768,640]{1,0:T(8,128)(2,1)}, bf16[768,256]{1,0:T(8,128)(2,1)})) %all-reduce.31.cloned.1.call-update) | async-done | bytes 1769488 | tf_op jit(solution)/shard_map/psum | solution.py:291
  373.4 233.6 %all-reduce.27.cloned.1.call-done = (f32[640,256]{1,0:T(8,128)}, f32[640,256]{1,0:T(8,128)}, f32[640,256]{1,0:T(8,128)}, f32[256,640]{0,1:T(8,128)}, f32[640,512...) async-done(((f32[640,256]{1,0:T(8,128)}, f32[640,256]{1,0:T(8,128)}, f32[640,256]{1,0:T(8,128)}, f32[256,640]{0,1:T(8,128)}, f32[640,512]{1,0:T(8,128)}, ...) | async-done | bytes 6553616 | tf_op jit(solution)/shard_map/psum | solution.py:313
  607.0 7.0 psum.245
  614.6 3.9 fusion.21
  618.5 16.7 %all-reduce.8 = (f32[640]{0:T(1024)S(1)}, f32[256]{0:T(256)S(1)}, f32[256]{0:T(256)S(1)}, f32[640]{0:T(1024)S(1)}, f32[640]{0:T(1024)S(1)}, /*index=5*/f32[640]{0:T(1024)S(1)}) all-reduce(f32[640]{0:T(1024)S(1)} %get-tuple-element.19, bf16[256]{0:T(256)(128)(2,1)S(1)} %psum.245, ...), channel_id=1, replica_groups=mesh['dp'=2,'context'=4,'tensor'=4] {'context'}, use_global_device_ids=true, to_apply=%region_37.38 | all-reduce | flops 3072 | bytes 24064 | tf_op jit(solution)/shard_map/psum | solution.py:313
  635.2 8.6 %all-reduce.10 = (f32[640]{0:T(1024)S(1)}, f32[256]{0:T(256)S(1)}, f32[256]{0:T(256)S(1)}, f32[640]{0:T(1024)S(1)}, f32[640]{0:T(1024)S(1)}, /*index=5*/f32[640]{0:T(1024)S(1)}) all-reduce(f32[640]{0:T(1024)S(1)} %get-tuple-element.36, f32[256]{0:T(256)S(1)} %get-tuple-element.37, ...), channel_id=1, replica_groups=mesh['dp'=2,'context'=4,'tensor'=4] {'dp'}, use_global_device_ids=true, to_apply=%region_38.39 | all-reduce | flops 3072 | bytes 24576 | tf_op jit(solution)/shard_map/psum | solution.py:312
  651.0 119.3 %all-reduce.29.cloned.1.call-done = (f32[640,256]{1,0:T(8,128)}, f32[640,256]{1,0:T(8,128)}, f32[640,256]{1,0:T(8,128)}, f32[256,640]{0,1:T(8,128)}, f32[640,512...) async-done(((f32[640,256]{1,0:T(8,128)}, f32[640,256]{1,0:T(8,128)}, f32[640,256]{1,0:T(8,128)}, f32[256,640]{0,1:T(8,128)}, f32[640,512]{1,0:T(8,128)}, ...) | async-done | bytes 6553616 | tf_op jit(solution)/shard_map/psum | solution.py:312
  (396 shorter events, 134.1 us)
Async XLA Ops:
  7.2 138.0 %all-reduce.21.cloned.1.call-start = ((), (), s32[]{:S(2)}) async-start(), calls=%async_computation | async-start | bytes 1966080 | tf_op jit(solution)/shard_map/psum | solution.py:199
  19.0 48.6 %copy-start.87 = (f32[640]{0:T(1024)}, f32[640]{0:T(1024)S(1)}, u32[]{:S(2)}) copy-start(f32[640]{0:T(1024)S(1)} %convert_element_type.203) | copy-start | bytes 7684
  20.6 47.0 %copy-start.89 = (f32[768]{0:T(1024)}, f32[768]{0:T(1024)S(1)}, u32[]{:S(2)}) copy-start(f32[768]{0:T(1024)S(1)} %fusion.124) | copy-start | bytes 9220
  29.5 41.9 %collective-permute-start.3 = (bf16[768,256]{1,0:T(8,128)(2,1)S(1)}, bf16[768,256]{1,0:T(8,128)(2,1)S(1)}, u32[]{:S(2)}, u32[]{:S(2)}) collective-permute-start(bf16[768,256]{1,0:T(8,128)(2,1)S(1)} %convolution_convert_fusion.5), channel_id=1, source_target_pairs={{0,4},{4,8},{8,12},{1,5},{5,9},{9,13},{2,6},{6,10},{10,14},{3,7},{... | collective-permute-start | bytes 1179656 | tf_op jit(solution)/shard_map/ppermute | solution.py:17
  33.5 35.0 %copy-start.114 = (f32[128]{0:T(128)}, f32[128]{0:T(128)S(1)}, u32[]{:S(2)}) copy-start(f32[128]{0:T(128)S(1)} %multiply_exponential_fusion) | copy-start | bytes 1540
  33.6 43.3 %copy-start.108 = (s32[768]{0:T(1024)}, s32[768]{0:T(1024)S(1)}, u32[]{:S(2)}) copy-start(s32[768]{0:T(1024)S(1)} %get-tuple-element.101) | copy-start | bytes 9220
  47.3 27.6 %collective-permute-start = (bf16[768,256]{0,1:T(8,128)(2,1)S(1)}, bf16[768,256]{0,1:T(8,128)(2,1)S(1)}, u32[]{:S(2)}, u32[]{:S(2)}) collective-permute-start(bf16[768,256]{0,1:T(8,128)(2,1)S(1)} %pad_maximum_fusion), channel_id=1, source_target_pairs={{0,4},{4,8},{8,12},{1,5},{5,9},{9,13},{2,6},{6,10},{10,14},{3,7},{... | collective-permute-start | bytes 1179656 | tf_op jit(solution)/shard_map/ppermute | solution.py:17
  67.6 39.3 %copy-start.27 = (bf16[256,640]{0,1:T(8,128)(2,1)}, bf16[256,640]{0,1:T(8,128)(2,1)S(1)}, u32[]{:S(2)}) copy-start(bf16[256,640]{0,1:T(8,128)(2,1)S(1)} %all_gather.45) | copy-start | bytes 983044
  70.2 31.6 %copy-start.68 = (bf16[768,128]{0,1:T(8,128)(2,1)}, bf16[768,128]{0,1:T(8,128)(2,1)S(1)}, u32[]{:S(2)}) copy-start(bf16[768,128]{0,1:T(8,128)(2,1)S(1)} %get-tuple-element.77) | copy-start | bytes 589828
  70.2 31.6 %copy-start.70 = (bf16[768,128]{0,1:T(8,128)(2,1)}, bf16[768,128]{0,1:T(8,128)(2,1)S(1)}, u32[]{:S(2)}) copy-start(bf16[768,128]{0,1:T(8,128)(2,1)S(1)} %get-tuple-element.78) | copy-start | bytes 589828
  71.0 32.7 %copy-start = (f32[1,768,768]{1,2,0:T(8,128)}, f32[1,768,768]{1,2,0:T(8,128)S(1)}, u32[]{:S(2)}) copy-start(f32[1,768,768]{1,2,0:T(8,128)S(1)} %get-tuple-element.96) | copy-start | bytes 7077892
  71.4 12.9 %collective-permute-start.4 = (bf16[768,256]{1,0:T(8,128)(2,1)S(1)}, bf16[768,256]{1,0:T(8,128)(2,1)S(1)}, u32[]{:S(2)}, u32[]{:S(2)}) collective-permute-start(bf16[768,256]{1,0:T(8,128)(2,1)S(1)} %collective-permute-done.3), channel_id=1, source_target_pairs={{0,4},{4,8},{8,12},{1,5},{5,9},{9,13},{2,6},{6,10},{10,14},{3,7},{... | collective-permute-start | bytes 1179656 | tf_op jit(solution)/shard_map/ppermute | solution.py:17
  74.9 17.2 %collective-permute-start.1 = (bf16[768,256]{0,1:T(8,128)(2,1)S(1)}, bf16[768,256]{0,1:T(8,128)(2,1)S(1)}, u32[]{:S(2)}, u32[]{:S(2)}) collective-permute-start(bf16[768,256]{0,1:T(8,128)(2,1)S(1)} %collective-permute-done), channel_id=1, source_target_pairs={{0,4},{4,8},{8,12},{1,5},{5,9},{9,13},{2,6},{6,10},{10,14},{3,7},{... | collective-permute-start | bytes 1179656 | tf_op jit(solution)/shard_map/ppermute | solution.py:17
  77.6 27.5 %copy-start.2 = (f32[1,768,768]{1,2,0:T(8,128)}, f32[1,768,768]{1,2,0:T(8,128)S(1)}, u32[]{:S(2)}) copy-start(f32[1,768,768]{1,2,0:T(8,128)S(1)} %get-tuple-element.94) | copy-start | bytes 7077892
  84.3 22.0 %collective-permute-start.5 = (bf16[768,256]{1,0:T(8,128)(2,1)S(1)}, bf16[768,256]{1,0:T(8,128)(2,1)S(1)}, u32[]{:S(2)}, u32[]{:S(2)}) collective-permute-start(bf16[768,256]{1,0:T(8,128)(2,1)S(1)} %collective-permute-done.4), channel_id=1, source_target_pairs={{0,4},{4,8},{8,12},{1,5},{5,9},{9,13},{2,6},{6,10},{10,14},{3,7},{... | collective-permute-start | bytes 1179656 | tf_op jit(solution)/shard_map/ppermute | solution.py:17
  92.1 9.7 %collective-permute-start.2 = (bf16[768,256]{0,1:T(8,128)(2,1)S(1)}, bf16[768,256]{0,1:T(8,128)(2,1)S(1)}, u32[]{:S(2)}, u32[]{:S(2)}) collective-permute-start(bf16[768,256]{0,1:T(8,128)(2,1)S(1)} %collective-permute-done.1), channel_id=1, source_target_pairs={{0,4},{4,8},{8,12},{1,5},{5,9},{9,13},{2,6},{6,10},{10,14},{3,7},{... | collective-permute-start | bytes 1179656 | tf_op jit(solution)/shard_map/ppermute | solution.py:17
  109.3 84.3 %all-reduce.23.cloned.1.call-start = ((), (), s32[]{:S(2)}) async-start(), calls=%async_computation.1 | async-start | bytes 1966080 | tf_op jit(solution)/shard_map/psum | solution.py:214
  157.5 83.9 %all-reduce.25.cloned.1.call-start = ((), (), s32[]{:S(2)}) async-start(), calls=%async_computation.2 | async-start | bytes 1966080 | tf_op jit(solution)/shard_map/psum | solution.py:228
  205.4 161.8 %all-reduce.31.cloned.1.call-start = ((), (), s32[]{:S(2)}) async-start(), calls=%async_computation.5 | async-start | bytes 3538944 | tf_op jit(solution)/shard_map/psum | solution.py:291
  265.6 13.9 %collective-permute-start.9 = (bf16[768,256]{1,0:T(8,128)(2,1)S(1)}, bf16[768,256]{1,0:T(8,128)(2,1)S(1)}, u32[]{:S(2)}, u32[]{:S(2)}) collective-permute-start(bf16[768,256]{1,0:T(8,128)(2,1)S(1)} %convolution_convert_fusion.3), channel_id=1, source_target_pairs={{4,0},{8,4},{12,8},{5,1},{9,5},{13,9},{6,2},{10,6},{14,10},{7,3},{... | collective-permute-start | bytes 1179656 | tf_op jit(solution)/shard_map/ppermute | solution.py:17
  271.3 16.7 %collective-permute-start.6 = (bf16[768,256]{0,1:T(8,128)(2,1)S(1)}, bf16[768,256]{0,1:T(8,128)(2,1)S(1)}, u32[]{:S(2)}, u32[]{:S(2)}) collective-permute-start(bf16[768,256]{0,1:T(8,128)(2,1)S(1)} %fusion.53), channel_id=1, source_target_pairs={{4,0},{8,4},{12,8},{5,1},{9,5},{13,9},{6,2},{10,6},{14,10},{7,3},{... | collective-permute-start | bytes 1179656 | tf_op jit(solution)/shard_map/ppermute | solution.py:17
  280.1 16.3 %collective-permute-start.10 = (bf16[768,256]{1,0:T(8,128)(2,1)S(1)}, bf16[768,256]{1,0:T(8,128)(2,1)S(1)}, u32[]{:S(2)}, u32[]{:S(2)}) collective-permute-start(bf16[768,256]{1,0:T(8,128)(2,1)S(1)} %add_convert_fusion.3), channel_id=1, source_target_pairs={{4,0},{8,4},{12,8},{5,1},{9,5},{13,9},{6,2},{10,6},{14,10},{7,3},{... | collective-permute-start | bytes 1179656 | tf_op jit(solution)/shard_map/ppermute | solution.py:17
  288.5 16.3 %collective-permute-start.7 = (bf16[768,256]{0,1:T(8,128)(2,1)S(1)}, bf16[768,256]{0,1:T(8,128)(2,1)S(1)}, u32[]{:S(2)}, u32[]{:S(2)}) collective-permute-start(bf16[768,256]{0,1:T(8,128)(2,1)S(1)} %add_convert_fusion.6), channel_id=1, source_target_pairs={{4,0},{8,4},{12,8},{5,1},{9,5},{13,9},{6,2},{10,6},{14,10},{7,3},{... | collective-permute-start | bytes 1179656 | tf_op jit(solution)/shard_map/ppermute | solution.py:17
  296.5 16.8 %collective-permute-start.11 = (bf16[768,256]{1,0:T(8,128)(2,1)S(1)}, bf16[768,256]{1,0:T(8,128)(2,1)S(1)}, u32[]{:S(2)}, u32[]{:S(2)}) collective-permute-start(bf16[768,256]{1,0:T(8,128)(2,1)S(1)} %add_convert_fusion.2), channel_id=1, source_target_pairs={{4,0},{8,4},{12,8},{5,1},{9,5},{13,9},{6,2},{10,6},{14,10},{7,3},{... | collective-permute-start | bytes 1179656 | tf_op jit(solution)/shard_map/ppermute | solution.py:17
  304.9 14.8 %collective-permute-start.8 = (bf16[768,256]{0,1:T(8,128)(2,1)S(1)}, bf16[768,256]{0,1:T(8,128)(2,1)S(1)}, u32[]{:S(2)}, u32[]{:S(2)}) collective-permute-start(bf16[768,256]{0,1:T(8,128)(2,1)S(1)} %add_convert_fusion.5), channel_id=1, source_target_pairs={{4,0},{8,4},{12,8},{5,1},{9,5},{13,9},{6,2},{10,6},{14,10},{7,3},{... | collective-permute-start | bytes 1179656 | tf_op jit(solution)/shard_map/ppermute | solution.py:17
  320.6 286.4 %all-reduce.27.cloned.1.call-start = ((), (), s32[]{:S(2)}) async-start(), calls=%async_computation.3 | async-start | bytes 13107200 | tf_op jit(solution)/shard_map/psum | solution.py:313
  328.3 41.6 %copy-start.18 = (f32[768,256]{0,1:T(8,128)S(1)}, f32[768,256]{0,1:T(8,128)}, u32[]{:S(2)}) copy-start(f32[768,256]{0,1:T(8,128)} %copy-done.17) | copy-start | bytes 2359300
  328.3 41.6 %copy-start.84 = (f32[768]{0:T(1024)S(1)}, f32[768]{0:T(1024)}, u32[]{:S(2)}) copy-start(f32[768]{0:T(1024)} %copy-done.83) | copy-start | bytes 9220
  328.3 41.6 %copy-start.99 = (f32[2,1,128]{2,1,0:T(1,128)S(1)}, f32[2,1,128]{2,1,0:T(1,128)}, u32[]{:S(2)}) copy-start(f32[2,1,128]{2,1,0:T(1,128)} %copy-done.98) | copy-start | bytes 3076
  373.3 397.0 %all-reduce.29.cloned.1.call-start = ((), (), s32[]{:S(2)}) async-start(), calls=%async_computation.4 | async-start | bytes 13107200 | tf_op jit(solution)/shard_map/psum | solution.py:312
  614.6 33.0 %copy-start.92 = (f32[768]{0:T(1024)S(1)}, f32[768]{0:T(1024)}, u32[]{:S(2)}) copy-start(f32[768]{0:T(1024)} %copy-done.91) | copy-start | bytes 9220
  614.6 33.0 %copy-start.10 = (f32[768,640]{1,0:T(8,128)S(1)}, f32[768,640]{1,0:T(8,128)}, u32[]{:S(2)}) copy-start(f32[768,640]{1,0:T(8,128)} %copy-done.9) | copy-start | bytes 5898244
  (107 other events, 584.1 us)
Sparse Core Ops, SparseCore 0:
  109.4 35.7 all-reduce.20
  157.6 35.9 all-reduce.22
  205.5 35.8 all-reduce.24
  320.7 46.3 all-reduce.30
  373.4 233.5 all-reduce.26
  609.9 160.3 all-reduce.28
